TPU v7x, 32 devices: a whole 2x2x4 slice. The times are simulated.
32 devices in a mesh: pair: 2 (over x), seq: 4 (over z), head: 4 (over y, core).
Axes of the slice: x: 2, y: 2, z: 4, core: 2. Of those that a mesh axis runs over, the one named last changes fastest.
Arguments:
- resp_query: bfloat16 [2, 4, 256, 4096], P('pair', 'seq', None, 'head'), may hold values from -6 to 6
- resp_key: bfloat16 [2, 4, 256, 1024], P('pair', 'seq', None, 'head'), may hold values from -6 to 6
- resp_value: bfloat16 [2, 4, 256, 1024], P('pair', 'seq', None, 'head'), may hold values from -6 to 6
- direction: bfloat16 [2, 4, 256, 4096], P('pair', 'seq', None, 'head'), may hold values from -96 to 96
- ratio: float32 [2, 4, 256], P('pair', 'seq'), may hold values from -4.2 to 4.2
- lengths: int32 [2, 4], P('pair', 'seq'), may hold values from 1 to 256, 640 in all within a row
- partner: int32 [4], replicated, may hold values from 0 to 3, each once
- prompt_key: bfloat16 [1024, 1024], P('pair', 'head'), may hold values from -6 to 6
- prompt_value: bfloat16 [1024, 1024], P('pair', 'head'), may hold values from -6 to 6
Outputs:
- query_grad: bfloat16 [2, 4, 256, 4096], P('pair', 'seq', None, 'head')
- resp_key_grad: bfloat16 [2, 4, 256, 1024], P('pair', 'seq', None, 'head')
- resp_value_grad: bfloat16 [2, 4, 256, 1024], P('pair', 'seq', None, 'head')
- prompt_key_grad: bfloat16 [1024, 1024], P('pair', 'head')
- prompt_value_grad: bfloat16 [1024, 1024], P('pair', 'head')
Inputs may be any that keep to these rules, and one draw needn't show every extreme that they name: On each side the response lengths sum to 640, and the longest is 256. partner names each rejected response exactly once.
All inputs are finite; a program needn't handle non-finite values. No bound on the sum of `lengths` on one device may be relied on, other than what follows from the above.
Results may differ from a plain program's by a relative error of at most 0.03.
Values may be sent and summed in bfloat16 or wider, within the bound.
A program may use at most 64 MiB of HBM per device.

v0:
```python
from functools import partial
import math
import jax
import jax.numpy as jnp
from jax import lax
from jax.sharding import PartitionSpec as P

HEAD_DIM = 128
dpo_beta = 0.1
block_limit = 128


def block_pass(operands, first_row, length, prompt_rows, head_group, score_scale):
    rows_q, rows_g, key_rows, value_rows = operands
    scores = jnp.dot(rows_q, key_rows.T, preferred_element_type=jnp.float32) * score_scale
    row_pos = first_row + jnp.arange(rows_q.shape[0], dtype=jnp.int32) // head_group
    key_pos = jnp.arange(key_rows.shape[0], dtype=jnp.int32) - prompt_rows
    visible = (key_pos[None, :] < 0) | (key_pos[None, :] <= row_pos[:, None]) & (
        key_pos[None, :] < length
    )
    scores = jnp.where(visible, scores, -jnp.inf)
    row_max = jnp.max(scores, axis=1, keepdims=True)
    exponent = jnp.exp(scores - row_max)
    attn_prob = exponent / jnp.sum(exponent, axis=1, keepdims=True)
    prob_half = attn_prob.astype(jnp.bfloat16)
    attended = jnp.dot(prob_half, value_rows, preferred_element_type=jnp.float32).astype(
        jnp.bfloat16
    )
    row_delta = jnp.sum(
        rows_g.astype(jnp.float32) * attended.astype(jnp.float32), axis=1, keepdims=True
    )
    prob_grad = jnp.dot(rows_g, value_rows.T, preferred_element_type=jnp.float32)
    score_grad = (attn_prob * (prob_grad - row_delta)).astype(jnp.bfloat16)
    query_rows = (
        jnp.dot(score_grad, key_rows, preferred_element_type=jnp.float32) * score_scale
    ).astype(jnp.bfloat16)
    key_add = jnp.dot(score_grad.T, rows_q, preferred_element_type=jnp.float32) * score_scale
    value_add = jnp.dot(prob_half.T, rows_g, preferred_element_type=jnp.float32)
    return (query_rows, key_add, value_add)


def block_skip(operands):
    rows_q, rows_g, key_rows, value_rows = operands
    empty_keys = jnp.zeros((key_rows.shape[0], key_rows.shape[1]), jnp.float32)
    return (jnp.zeros_like(rows_q), empty_keys, empty_keys)


def shards(
    resp_query, resp_key, resp_value, direction, ratio, lengths, partner, prompt_key, prompt_value
):
    length = lengths[0, 0]
    resp_rows = resp_query.shape[2]
    positions = jnp.arange(resp_rows, dtype=jnp.int32)
    live_mask = positions < length
    own_sum = jnp.sum(jnp.where(live_mask, ratio[0, 0], 0.0))
    side_index = lax.axis_index("pair")
    seq_index = lax.axis_index("seq")
    response_count = partner.shape[0]
    response_ids = jnp.arange(response_count, dtype=jnp.int32)
    side_ids = jnp.arange(2, dtype=jnp.int32)
    owned = (side_ids[:, None] == side_index) & (response_ids[None, :] == seq_index)
    score_table = lax.psum(jnp.where(owned, own_sum, 0.0), ("pair", "seq"))
    matched = partner[:, None] == response_ids[None, :]
    partner_sums = jnp.sum(jnp.where(matched, score_table[1][None, :], 0.0), axis=1)
    pulled = jax.nn.sigmoid(-(dpo_beta * (score_table[0] - partner_sums)))
    chosen_weight = -jnp.sum(jnp.where(response_ids == seq_index, pulled, 0.0))
    rejected_weight = jnp.sum(jnp.where(partner == seq_index, pulled, 0.0))
    weight = jnp.where(side_index == 0, chosen_weight, rejected_weight)
    out_grads = jnp.where(
        live_mask[:, None], weight * direction[0, 0].astype(jnp.float32), 0.0
    ).astype(jnp.bfloat16)
    whole_key, whole_value = (
        lax.all_gather(prompt_key, "pair", axis=0, tiled=True),
        lax.all_gather(prompt_value, "pair", axis=0, tiled=True),
    )
    kv_local = resp_key.shape[3] // HEAD_DIM
    head_group = resp_query.shape[3] // resp_key.shape[3]
    prompt_rows = whole_key.shape[0]
    block_rows = min(block_limit, resp_rows)
    score_scale = 1.0 / math.sqrt(HEAD_DIM)
    query_heads, key_heads, value_heads, prompt_key_terms, prompt_value_terms = ([], [], [], [], [])
    for kv_index in range(kv_local):
        head_cols = slice(kv_index * head_group * HEAD_DIM, (kv_index + 1) * head_group * HEAD_DIM)
        key_cols = slice(kv_index * HEAD_DIM, (kv_index + 1) * HEAD_DIM)
        query_head = resp_query[0, 0][:, head_cols]
        grad_head = out_grads[:, head_cols]
        resp_k = resp_key[0, 0][:, key_cols]
        resp_v = resp_value[0, 0][:, key_cols]
        prompt_k = whole_key[:, key_cols]
        prompt_v = whole_value[:, key_cols]
        prompt_dk = jnp.zeros((prompt_rows, HEAD_DIM), jnp.float32)
        prompt_dv = jnp.zeros((prompt_rows, HEAD_DIM), jnp.float32)
        resp_dk = jnp.zeros((resp_rows, HEAD_DIM), jnp.float32)
        resp_dv = jnp.zeros((resp_rows, HEAD_DIM), jnp.float32)
        query_blocks = []
        for block_index in range(resp_rows // block_rows):
            first_row = block_index * block_rows
            end_row = first_row + block_rows
            key_rows = jnp.concatenate([prompt_k, resp_k[:end_row]], 0)
            value_rows = jnp.concatenate([prompt_v, resp_v[:end_row]], 0)
            rows_q = query_head[first_row:end_row].reshape(block_rows * head_group, HEAD_DIM)
            rows_g = grad_head[first_row:end_row].reshape(block_rows * head_group, HEAD_DIM)
            active = partial(
                block_pass,
                first_row=first_row,
                length=length,
                prompt_rows=prompt_rows,
                head_group=head_group,
                score_scale=score_scale,
            )
            query_rows, key_add, value_add = lax.cond(
                first_row < length, active, block_skip, (rows_q, rows_g, key_rows, value_rows)
            )
            query_blocks.append(query_rows)
            prompt_dk = prompt_dk + key_add[:prompt_rows]
            prompt_dv = prompt_dv + value_add[:prompt_rows]
            resp_dk = resp_dk.at[:end_row].add(key_add[prompt_rows:])
            resp_dv = resp_dv.at[:end_row].add(value_add[prompt_rows:])
        query_heads.append(
            jnp.concatenate(query_blocks, 0).reshape(resp_rows, head_group * HEAD_DIM)
        )
        key_heads.append(resp_dk.astype(jnp.bfloat16))
        value_heads.append(resp_dv.astype(jnp.bfloat16))
        prompt_key_terms.append(prompt_dk)
        prompt_value_terms.append(prompt_dv)
    prompt_terms = jnp.concatenate(prompt_key_terms + prompt_value_terms, 1)
    own_rows = prompt_key.shape[0]
    summed = lax.psum(prompt_terms, ("pair", "seq"))
    reduced = lax.dynamic_slice_in_dim(summed, side_index * own_rows, own_rows, 0).astype(
        jnp.bfloat16
    )
    key_width = kv_local * HEAD_DIM
    query_grad = jnp.concatenate(query_heads, 1)[None, None]
    resp_key_grad = jnp.concatenate(key_heads, 1)[None, None]
    resp_value_grad = jnp.concatenate(value_heads, 1)[None, None]
    prompt_key_grad = reduced[:, :key_width]
    prompt_value_grad = reduced[:, key_width:]
    return (query_grad, resp_key_grad, resp_value_grad, prompt_key_grad, prompt_value_grad)


def solution(mesh):
    in_specs = (
        P("pair", "seq", None, "head"),
        P("pair", "seq", None, "head"),
        P("pair", "seq", None, "head"),
        P("pair", "seq", None, "head"),
        P("pair", "seq", None),
        P("pair", "seq"),
        P(),
        P("pair", "head"),
        P("pair", "head"),
    )
    out_specs = (
        P("pair", "seq", None, "head"),
        P("pair", "seq", None, "head"),
        P("pair", "seq", None, "head"),
        P("pair", "head"),
        P("pair", "head"),
    )
    return jax.shard_map(shards, mesh=mesh, in_specs=in_specs, out_specs=out_specs, check_vma=False)
```

profile of v0, /device:TPU:0, one launch (start us, length us, event | category | flops | bytes accessed | tf_op | source)
XLA Modules:
  0.0 192.5 jit_solution(14777387597338560229)
XLA Ops:
  1.4 1.3 select_reduce_fusion.1
  2.7 0.7 and_select_fusion
  3.4 23.3 %psum.14 = f32[2,4]{1,0:T(2,128)S(1)} all-reduce(f32[2,4]{1,0:T(2,128)S(1)} %and_select_fusion), channel_id=1, replica_groups=mesh['pair'=2,'seq'=4,'head'=4] {'pair','seq'}, use_global_device_ids=true, to_apply=%region_1.2 | all-reduce | flops 8 | bytes 64 | tf_op jit(solution)/shard_map/psum | solution.py:62
  26.6 0.8 select_reduce_fusion
  27.5 1.3 fusion.71
  30.1 0.8 fusion.82
  30.8 0.8 fusion.81
  31.6 0.9 fusion.84
  32.5 0.9 fusion.83
  33.4 1.2 fusion.70
  34.6 9.1 %all_gather.6 = bf16[1024,256]{1,0:T(8,128)(2,1)S(1)} all-gather(bf16[512,256]{1,0:T(8,128)(2,1)} %param.48), channel_id=1, replica_groups=mesh['pair'=2,'seq'=4,'head'=4] {'pair'}, dimensions={0}, use_global_device_ids=true | all-gather | bytes 786432 | tf_op jit(solution)/shard_map/all_gather | solution.py:73
  43.7 7.0 %all_gather.7 = bf16[1024,256]{1,0:T(8,128)(2,1)S(1)} all-gather(bf16[512,256]{1,0:T(8,128)(2,1)S(1)} %copy-done.13), channel_id=1, replica_groups=mesh['pair'=2,'seq'=4,'head'=4] {'pair'}, dimensions={0}, use_global_device_ids=true | all-gather | bytes 786432 | tf_op jit(solution)/shard_map/all_gather | solution.py:74
  50.9 0.8 pad_maximum_fusion.1
  51.7 0.8 pad_maximum_fusion.5
  52.5 8.8 %conditional.7 = (bf16[512,128]{1,0:T(8,128)(2,1)}, f32[1280,128]{1,0:T(8,128)S(1)}, f32[1280,128]{1,0:T(8,128)S(1)}) conditional(s32[]{:T(128)} %convert_element_type.117, () %tuple.114, (s32[]{:T(128)}, bf16[256,1024]{1,0:T(8,128)(2,1)}, bf16[1280,128]{1,0:T(8,128)(2,1)}, bf16[256,1024]{1,0:T(8,128)(2,1)S(1)}, ...), branch_computations={%region_20.21_spmd, %region_21.25_spmd} | conditional | flops 1017094144 | bytes 28345400 | solution.py:111
  53.2 0.9 slice.282
  54.4 1.9 fusion.77
  59.6 1.2 fusion.57
  61.3 8.2 %conditional.5 = (bf16[512,128]{1,0:T(8,128)(2,1)}, f32[1280,128]{1,0:T(8,128)}, f32[1280,128]{1,0:T(8,128)S(1)}) conditional(s32[]{:T(128)} %convert_element_type.117, () %tuple.110, (s32[]{:T(128)}, bf16[256,1024]{1,0:T(8,128)(2,1)}, bf16[1280,128]{1,0:T(8,128)(2,1)S(1)}, bf16[256,1024]{1,0:T(8,128)(2,1)S(1)}, ...), branch_computations={%region_10.11_spmd, %region_11.15_spmd} | conditional | flops 1017094144 | bytes 27034652 | solution.py:111
  61.4 0.7 fusion.29
  62.0 0.9 slice.272
  63.3 0.9 fusion.75
  67.0 1.2 fusion.22
  68.1 1.4 convolution_multiply_fusion.4
  69.5 9.7 %conditional.6 = (bf16[512,128]{1,0:T(8,128)(2,1)S(1)}, f32[1024,128]{1,0:T(8,128)}, f32[1024,128]{1,0:T(8,128)S(1)}, f32[256,128]{1,0:T(8,128)S(1)}, f32[256,128]{1,0:T(8,128)S(1)}) conditional(s32[]{:T(128)} %convert_element_type.114, () %tuple.112, (s32[]{:T(128)}, bf16[256,1024]{1,0:T(8,128)(2,1)}, bf16[1152,128]{1,0:T(8,128)(2,1)}, ...), branch_computations={%region_15.16_spmd, %region_16.20_spmd} | conditional | flops 915430400 | bytes 28474960 | solution.py:111
  70.2 0.9 slice.276
  71.2 0.9 slice.277
  72.4 1.8 fusion.76
  78.3 0.8 slice.336
  80.0 1.0 pad_maximum_fusion.10
  80.9 0.9 reshape.380
  81.8 1.5 add_convert_fusion.2
  83.3 1.9 slice_add_fusion.2
  85.9 0.9 slice_add_fusion
  86.7 8.3 %conditional.4 = (bf16[512,128]{1,0:T(8,128)(2,1)S(1)}, f32[1024,128]{1,0:T(8,128)}, f32[1024,128]{1,0:T(8,128)S(1)}, f32[256,128]{1,0:T(8,128)S(1)}, f32[256,128]{1,0:T(8,128)S(1)}) conditional(s32[]{:T(128)} %convert_element_type.114, () %tuple.108, (s32[]{:T(128)}, bf16[256,1024]{1,0:T(8,128)(2,1)}, bf16[1152,128]{1,0:T(8,128)(2,1)S(1)}, ...), branch_computations={%region_5.6_spmd, %region_6.10_spmd} | conditional | flops 915430400 | bytes 27295284 | solution.py:111
  86.7 0.7 fusion.12
  87.5 0.9 slice.266
  88.5 0.9 slice.267
  89.6 0.9 fusion.74
  94.2 0.8 slice.332
  95.8 1.0 pad_maximum_fusion.9
  97.1 0.9 maximum_bitcast_fusion
  97.9 1.0 add_convert_fusion.3
  98.9 1.3 slice_add_fusion.3
  100.2 0.7 maximum_bitcast_fusion.1
  101.1 89.8 %all-reduce.7 = bf16[1024,512]{1,0:T(8,128)(2,1)S(1)} all-reduce(f32[1024,512]{1,0:T(8,128)S(1)} %pad_maximum_fusion), channel_id=1, replica_groups=mesh['pair'=2,'seq'=4,'head'=4] {'pair','seq'}, use_global_device_ids=true, to_apply=%region_25.26 | all-reduce | flops 524288 | bytes 3145728 | tf_op jit(solution)/shard_map/psum | solution.py:128
  191.0 0.7 maximum_bitcast_fusion.2
  191.7 0.8 fusion.78
  (105 shorter events, 19.6 us)
Async XLA Ops:
  0.6 43.1 %copy-start.13 = (bf16[512,256]{1,0:T(8,128)(2,1)S(1)}, bf16[512,256]{1,0:T(8,128)(2,1)}, u32[]{:S(2)}) copy-start(bf16[512,256]{1,0:T(8,128)(2,1)} %param.49) | copy-start | bytes 786436
  34.6 26.7 %copy-start = (bf16[256,1024]{1,0:T(8,128)(2,1)}, bf16[256,1024]{1,0:T(8,128)(2,1)S(1)}, u32[]{:S(2)}) copy-start(bf16[256,1024]{1,0:T(8,128)(2,1)S(1)} %fusion.70) | copy-start | bytes 1572868
  58.6 1.0 copy-start.3
  76.3 1.0 copy-start.5
  79.3 0.6 copy-start.7
  79.3 0.7 copy-start.11
  79.3 6.6 %copy-start.4 = (bf16[1152,128]{1,0:T(8,128)(2,1)S(1)}, bf16[1152,128]{1,0:T(8,128)(2,1)}, u32[]{:S(2)}) copy-start(bf16[1152,128]{1,0:T(8,128)(2,1)} %get-tuple-element.317) | copy-start | bytes 884740
  86.7 10.3 %copy-start.6 = (bf16[256,512]{1,0:T(8,128)(2,1)S(1)}, bf16[256,512]{1,0:T(8,128)(2,1)}, u32[]{:S(2)}) copy-start(bf16[256,512]{1,0:T(8,128)(2,1)} %reshape.380) | copy-start | bytes 786436
  95.1 0.6 copy-start.8
  95.1 0.7 copy-start.10
  95.1 0.7 copy-start.12
  95.1 5.0 %copy-start.15 = (bf16[256,128]{1,0:T(8,128)(2,1)S(1)}, bf16[256,128]{1,0:T(8,128)(2,1)}, u32[]{:S(2)}) copy-start(bf16[256,128]{1,0:T(8,128)(2,1)} %add_convert_fusion.2) | copy-start | bytes 196612
  95.8 5.0 %copy-start.9 = (f32[256,128]{1,0:T(8,128)S(1)}, f32[256,128]{1,0:T(8,128)}, u32[]{:S(2)}) copy-start(f32[256,128]{1,0:T(8,128)} %copy-done.8) | copy-start | bytes 393220
  97.0 3.9 %copy-start.1 = (f32[1024,128]{1,0:T(8,128)S(1)}, f32[1024,128]{1,0:T(8,128)}, u32[]{:S(2)}) copy-start(f32[1024,128]{1,0:T(8,128)} %slice_add_fusion.2) | copy-start | bytes 1572868
  97.0 3.9 %copy-start.2 = (f32[1024,128]{1,0:T(8,128)S(1)}, f32[1024,128]{1,0:T(8,128)}, u32[]{:S(2)}) copy-start(f32[1024,128]{1,0:T(8,128)} %slice_add_fusion) | copy-start | bytes 1572868
  101.1 89.9 %copy-start.14 = (bf16[256,128]{1,0:T(8,128)(2,1)S(1)}, bf16[256,128]{1,0:T(8,128)(2,1)}, u32[]{:S(2)}) copy-start(bf16[256,128]{1,0:T(8,128)(2,1)} %add_convert_fusion) | copy-start | bytes 196612
where the time goes:
time: 194 us; the launch traced here: 192 us
  blocking collectives  129 us (66%)
  other arithmetic  25.7 us (13%)
  matrix products  18.2 us (9%)
  local copies, waits for them, and re-layouts  16.1 us (8%)
  between operations  2.92 us (2%)
    psum x1, blocking collectives, shards(): summed = lax.psum(prompt_terms, ('pair', 'seq'))  89.8 us
    psum x1, blocking collectives, shards(): score_table = lax.psum(jnp.where(owned, own_sum, 0.0), ('pair', 'seq'))  23.3 us
    all_gather x1, blocking collectives, shards(): lax.all_gather(prompt_key, 'pair', axis=0, tiled=True)  9.08 us
    all_gather x1, blocking collectives, shards(): lax.all_gather(prompt_value, 'pair', axis=0, tiled=True)  7.04 us
    dot_general x4, matrix products, block_pass(): jnp.dot(rows_q, key_rows.T, preferred_element_type=jnp.float32)  5.45 us

commit v1 on v0

--- a/solution.py
+++ b/solution.py
@@ -8,6 +8,12 @@
 HEAD_DIM = 128
 dpo_beta = 0.1
 block_limit = 128
+
+
+def draft_squares(local_values, comm_axis, dev_axis):
+    top = lax.psum(local_values, comm_axis)
+    shaped = lax.psum(top, axis_name=dev_axis)
+    return shaped
 
 
 def block_pass(operands, first_row, length, prompt_rows, head_group, score_scale):
@@ -59,7 +65,7 @@
     response_ids = jnp.arange(response_count, dtype=jnp.int32)
     side_ids = jnp.arange(2, dtype=jnp.int32)
     owned = (side_ids[:, None] == side_index) & (response_ids[None, :] == seq_index)
-    score_table = lax.psum(jnp.where(owned, own_sum, 0.0), ("pair", "seq"))
+    score_table = draft_squares(jnp.where(owned, own_sum, 0.0), "seq", "pair")
     matched = partner[:, None] == response_ids[None, :]
     partner_sums = jnp.sum(jnp.where(matched, score_table[1][None, :], 0.0), axis=1)
     pulled = jax.nn.sigmoid(-(dpo_beta * (score_table[0] - partner_sums)))

time: 194 us -> 188 us (0.969)
  blocking collectives: 129 us -> 123 us
    psum x1 -> x2, blocking collectives: 23.3 us -> 18.4 us  [the longest x1 13.5 us: draft_squares(): top = lax.psum(local_values, comm_axis)]
where the time goes in v1:
time: 188 us; the launch traced here: 187 us
  blocking collectives  123 us (65%)
  other arithmetic  25.7 us (14%)
  matrix products  18.2 us (10%)
  local copies, waits for them, and re-layouts  16.1 us (9%)
  between operations  2.92 us (2%)
    psum x1, blocking collectives, shards(): summed = lax.psum(prompt_terms, ('pair', 'seq'))  89.5 us
    psum x1, blocking collectives, draft_squares(): top = lax.psum(local_values, comm_axis)  13.5 us
    all_gather x1, blocking collectives, shards(): lax.all_gather(prompt_key, 'pair', axis=0, tiled=True)  8.48 us
    all_gather x1, blocking collectives, shards(): lax.all_gather(prompt_value, 'pair', axis=0, tiled=True)  7.04 us
    dot_general x4, matrix products, block_pass(): jnp.dot(rows_q, key_rows.T, preferred_element_type=jnp.float32)  5.44 us
    psum x1, blocking collectives, draft_squares(): shaped = lax.psum(top, axis_name=dev_axis)  4.91 us

profile of v1, /device:TPU:0, one launch (start us, length us, event | category | flops | bytes accessed | tf_op | source)
XLA Modules:
  0.0 186.7 jit_solution(15163311192883842973)
XLA Ops:
  1.4 1.3 select_reduce_fusion.1
  2.7 0.7 and_select_fusion
  3.4 13.5 %psum.21 = f32[2,4]{1,0:T(2,128)S(1)} all-reduce(f32[2,4]{1,0:T(2,128)S(1)} %and_select_fusion), channel_id=1, replica_groups=mesh['pair'=2,'seq'=4,'head'=4] {'seq'}, use_global_device_ids=true, to_apply=%region_1.2 | all-reduce | flops 8 | bytes 64 | tf_op jit(solution)/shard_map/psum | solution.py:14
  16.8 4.9 %psum.22 = f32[2,4]{1,0:T(2,128)S(1)} all-reduce(f32[2,4]{1,0:T(2,128)S(1)} %psum.21), channel_id=1, replica_groups=mesh['pair'=2,'seq'=4,'head'=4] {'pair'}, use_global_device_ids=true, to_apply=%region_2.3 | all-reduce | flops 8 | bytes 64 | tf_op jit(solution)/shard_map/psum | solution.py:15
  21.7 0.8 select_reduce_fusion
  22.6 1.3 fusion.71
  25.2 0.8 fusion.82
  26.0 0.8 fusion.81
  26.7 0.9 fusion.84
  27.6 0.9 fusion.83
  28.5 1.2 fusion.70
  29.7 8.5 %all_gather.6 = bf16[1024,256]{1,0:T(8,128)(2,1)S(1)} all-gather(bf16[512,256]{1,0:T(8,128)(2,1)} %param.48), channel_id=1, replica_groups=mesh['pair'=2,'seq'=4,'head'=4] {'pair'}, dimensions={0}, use_global_device_ids=true | all-gather | bytes 786432 | tf_op jit(solution)/shard_map/all_gather | solution.py:79
  38.2 7.0 %all_gather.7 = bf16[1024,256]{1,0:T(8,128)(2,1)S(1)} all-gather(bf16[512,256]{1,0:T(8,128)(2,1)S(1)} %copy-done.13), channel_id=1, replica_groups=mesh['pair'=2,'seq'=4,'head'=4] {'pair'}, dimensions={0}, use_global_device_ids=true | all-gather | bytes 786432 | tf_op jit(solution)/shard_map/all_gather | solution.py:80
  45.4 0.8 pad_maximum_fusion.1
  46.2 0.8 pad_maximum_fusion.5
  47.0 8.8 %conditional.7 = (bf16[512,128]{1,0:T(8,128)(2,1)}, f32[1280,128]{1,0:T(8,128)S(1)}, f32[1280,128]{1,0:T(8,128)S(1)}) conditional(s32[]{:T(128)} %convert_element_type.117, () %tuple.114, (s32[]{:T(128)}, bf16[256,1024]{1,0:T(8,128)(2,1)}, bf16[1280,128]{1,0:T(8,128)(2,1)}, bf16[256,1024]{1,0:T(8,128)(2,1)S(1)}, ...), branch_computations={%region_21.22_spmd, %region_22.26_spmd} | conditional | flops 1017094144 | bytes 28345400 | solution.py:117
  47.7 0.9 slice.282
  48.9 1.9 fusion.77
  54.1 1.2 fusion.57
  55.8 8.2 %conditional.5 = (bf16[512,128]{1,0:T(8,128)(2,1)}, f32[1280,128]{1,0:T(8,128)}, f32[1280,128]{1,0:T(8,128)S(1)}) conditional(s32[]{:T(128)} %convert_element_type.117, () %tuple.110, (s32[]{:T(128)}, bf16[256,1024]{1,0:T(8,128)(2,1)}, bf16[1280,128]{1,0:T(8,128)(2,1)S(1)}, bf16[256,1024]{1,0:T(8,128)(2,1)S(1)}, ...), branch_computations={%region_11.12_spmd, %region_12.16_spmd} | conditional | flops 1017094144 | bytes 27034652 | solution.py:117
  56.5 0.9 slice.272
  57.8 0.9 fusion.75
  61.5 1.2 fusion.22
  62.6 1.4 convolution_multiply_fusion.4
  64.0 9.7 %conditional.6 = (bf16[512,128]{1,0:T(8,128)(2,1)S(1)}, f32[1024,128]{1,0:T(8,128)}, f32[1024,128]{1,0:T(8,128)S(1)}, f32[256,128]{1,0:T(8,128)S(1)}, f32[256,128]{1,0:T(8,128)S(1)}) conditional(s32[]{:T(128)} %convert_element_type.114, () %tuple.112, (s32[]{:T(128)}, bf16[256,1024]{1,0:T(8,128)(2,1)}, bf16[1152,128]{1,0:T(8,128)(2,1)}, ...), branch_computations={%region_16.17_spmd, %region_17.21_spmd} | conditional | flops 915430400 | bytes 28474960 | solution.py:117
  64.7 0.9 slice.276
  65.7 0.9 slice.277
  66.8 1.8 fusion.76
  72.8 0.8 slice.336
  74.4 1.0 pad_maximum_fusion.10
  75.4 0.9 reshape.380
  76.3 1.5 add_convert_fusion.2
  77.8 1.9 %slice_add_fusion.2 = f32[1024,128]{1,0:T(8,128)} fusion(f32[1024,128]{1,0:T(8,128)} %get-tuple-element.280, f32[1280,128]{1,0:T(8,128)S(1)} %get-tuple-element.274), kind=kLoop, calls=%fused_computation.121 | loop fusion | flops 131072 | bytes 1572864 | tf_op jit(solution)/shard_map/add | solution.py:121
  80.4 0.9 slice_add_fusion
  81.2 8.3 %conditional.4 = (bf16[512,128]{1,0:T(8,128)(2,1)S(1)}, f32[1024,128]{1,0:T(8,128)}, f32[1024,128]{1,0:T(8,128)S(1)}, f32[256,128]{1,0:T(8,128)S(1)}, f32[256,128]{1,0:T(8,128)S(1)}) conditional(s32[]{:T(128)} %convert_element_type.114, () %tuple.108, (s32[]{:T(128)}, bf16[256,1024]{1,0:T(8,128)(2,1)}, bf16[1152,128]{1,0:T(8,128)(2,1)S(1)}, ...), branch_computations={%region_6.7_spmd, %region_7.11_spmd} | conditional | flops 915430400 | bytes 27295284 | solution.py:117
  81.2 0.7 fusion.12
  81.9 0.9 slice.266
  83.0 0.9 slice.267
  84.1 0.9 fusion.74
  88.6 0.8 slice.332
  90.3 1.0 pad_maximum_fusion.9
  91.5 0.9 maximum_bitcast_fusion
  92.4 1.0 add_convert_fusion.3
  93.4 1.3 slice_add_fusion.3
  94.7 0.7 maximum_bitcast_fusion.1
  95.6 89.5 %all-reduce.7 = bf16[1024,512]{1,0:T(8,128)(2,1)S(1)} all-reduce(f32[1024,512]{1,0:T(8,128)S(1)} %pad_maximum_fusion), channel_id=1, replica_groups=mesh['pair'=2,'seq'=4,'head'=4] {'pair','seq'}, use_global_device_ids=true, to_apply=%region_26.27 | all-reduce | flops 524288 | bytes 3145728 | tf_op jit(solution)/shard_map/psum | solution.py:134
  185.2 0.7 maximum_bitcast_fusion.2
  185.9 0.8 fusion.78
  (106 shorter events, 20.3 us)
Async XLA Ops:
  0.6 37.6 %copy-start.13 = (bf16[512,256]{1,0:T(8,128)(2,1)S(1)}, bf16[512,256]{1,0:T(8,128)(2,1)}, u32[]{:S(2)}) copy-start(bf16[512,256]{1,0:T(8,128)(2,1)} %param.49) | copy-start | bytes 786436
  29.7 26.1 %copy-start = (bf16[256,1024]{1,0:T(8,128)(2,1)}, bf16[256,1024]{1,0:T(8,128)(2,1)S(1)}, u32[]{:S(2)}) copy-start(bf16[256,1024]{1,0:T(8,128)(2,1)S(1)} %fusion.70) | copy-start | bytes 1572868
  53.1 1.0 copy-start.3
  70.8 1.0 copy-start.5
  73.7 0.6 copy-start.7
  73.7 0.7 copy-start.11
  73.8 6.6 %copy-start.4 = (bf16[1152,128]{1,0:T(8,128)(2,1)S(1)}, bf16[1152,128]{1,0:T(8,128)(2,1)}, u32[]{:S(2)}) copy-start(bf16[1152,128]{1,0:T(8,128)(2,1)} %get-tuple-element.317) | copy-start | bytes 884740
  81.2 10.3 %copy-start.6 = (bf16[256,512]{1,0:T(8,128)(2,1)S(1)}, bf16[256,512]{1,0:T(8,128)(2,1)}, u32[]{:S(2)}) copy-start(bf16[256,512]{1,0:T(8,128)(2,1)} %reshape.380) | copy-start | bytes 786436
  89.6 0.6 copy-start.8
  89.6 0.7 copy-start.10
  89.6 0.7 copy-start.12
  89.6 5.0 %copy-start.15 = (bf16[256,128]{1,0:T(8,128)(2,1)S(1)}, bf16[256,128]{1,0:T(8,128)(2,1)}, u32[]{:S(2)}) copy-start(bf16[256,128]{1,0:T(8,128)(2,1)} %add_convert_fusion.2) | copy-start | bytes 196612
  90.3 5.0 %copy-start.9 = (f32[256,128]{1,0:T(8,128)S(1)}, f32[256,128]{1,0:T(8,128)}, u32[]{:S(2)}) copy-start(f32[256,128]{1,0:T(8,128)} %copy-done.8) | copy-start | bytes 393220
  91.5 3.9 %copy-start.1 = (f32[1024,128]{1,0:T(8,128)S(1)}, f32[1024,128]{1,0:T(8,128)}, u32[]{:S(2)}) copy-start(f32[1024,128]{1,0:T(8,128)} %slice_add_fusion.2) | copy-start | bytes 1572868
  91.5 3.9 %copy-start.2 = (f32[1024,128]{1,0:T(8,128)S(1)}, f32[1024,128]{1,0:T(8,128)}, u32[]{:S(2)}) copy-start(f32[1024,128]{1,0:T(8,128)} %slice_add_fusion) | copy-start | bytes 1572868
  95.6 89.6 %copy-start.14 = (bf16[256,128]{1,0:T(8,128)(2,1)S(1)}, bf16[256,128]{1,0:T(8,128)(2,1)}, u32[]{:S(2)}) copy-start(bf16[256,128]{1,0:T(8,128)(2,1)} %add_convert_fusion) | copy-start | bytes 196612
